TPU v7x, 32 devices: a whole 2x2x4 slice. The times are simulated.
32 devices in a mesh: probe: 4 (over y, core), store: 8 (over z, x).
Axes of the slice: x: 2, y: 2, z: 4, core: 2. Of those that a mesh axis runs over, the one named last changes fastest.
Arguments:
- probe_field: bfloat16 [96, 128, 8, 128], P('probe', 'store'), may hold values from -6 to 6
- bounds: int32 [96, 2], P('probe'), may hold values from 0 to 128, as said below
- courant: float32 [128, 8, 128], P('store'), may hold values from 0.1 to 0.2
- snapshots: bfloat16 [8, 128, 8, 128], P(None, 'store', 'probe'), may hold values from -0.5 to 0.5
- snap_times: int32 [8], replicated, may hold values from 0 to 7, each once
- basis_panels: bfloat16 [96, 128, 8, 128], P('probe', 'store'), may hold values from -0.015625 to 0.015625
Outputs:
- response: float32 [96, 128, 8, 128], P('probe', 'store')
- projection: float32 [96, 96], P(None, 'probe')
Inputs may be any that keep to these rules, and one draw needn't show every extreme that they name: 0 <= bounds[k, 0] < bounds[k, 1] <= 128 for every probe k, and each region holds at least 32 rows.
All inputs are finite; a program needn't handle non-finite values.
Results may differ from a plain program's by a relative error of at most 0.0031.
Values may be sent and summed in bfloat16 or wider, within the bound.
No kernel may reach another device: no remote copies, remote signals or barrier semaphores. Data moves between devices by JAX's collectives and lax.ppermute only.
A program may use at most 64 MiB of HBM per device.

v0:
```python
import jax
import jax.numpy as jnp
from jax import lax
from jax.sharding import PartitionSpec as P

stencil_taps = (-205.0 / 72.0, 8.0 / 5.0, -1.0 / 5.0, 8.0 / 315.0, -1.0 / 560.0)


def extended(x, sides, width):
    for axis, dim in sides:
        devices, length = (lax.axis_size(axis), x.shape[dim])
        up = [(i, (i + 1) % devices) for i in range(devices - 1)]
        down = [(j, i) for i, j in up]
        last = lax.slice_in_dim(x, length - width, length, axis=dim)
        leading = lax.slice_in_dim(x, 0, width, axis=dim)
        before = lax.ppermute(last, axis, up)
        after = lax.ppermute(leading, axis, down)
        x = jnp.concatenate([before, x, after], axis=dim)
    return x


def laplace(full):
    extent_x = full.shape[-3] - 8
    extent_y = full.shape[-2] - 8
    extent_z = full.shape[-1] - 8
    centre = full[..., 4 : 4 + extent_x, 4 : 4 + extent_y, 4 : 4 + extent_z]
    totals = 3.0 * stencil_taps[0] * centre
    for distance in range(1, 5):
        along = full[
            ..., 4 + distance : 4 + distance + extent_x, 4 : 4 + extent_y, 4 : 4 + extent_z
        ]
        along = (
            along
            + full[..., 4 - distance : 4 - distance + extent_x, 4 : 4 + extent_y, 4 : 4 + extent_z]
        )
        along = (
            along
            + full[..., 4 : 4 + extent_x, 4 + distance : 4 + distance + extent_y, 4 : 4 + extent_z]
        )
        along = (
            along
            + full[..., 4 : 4 + extent_x, 4 - distance : 4 - distance + extent_y, 4 : 4 + extent_z]
        )
        along = (
            along
            + full[..., 4 : 4 + extent_x, 4 : 4 + extent_y, 4 + distance : 4 + distance + extent_z]
        )
        along = (
            along
            + full[..., 4 : 4 + extent_x, 4 : 4 + extent_y, 4 - distance : 4 - distance + extent_z]
        )
        totals = totals + stencil_taps[distance] * along
    return totals


def slab_mask(row_index, bounds):
    return ((row_index[None, :] >= bounds[:, 0:1]) & (row_index[None, :] < bounds[:, 1:2])).astype(
        jnp.float32
    )


def side_frame(field):
    return jnp.pad(field, ((0, 0), (0, 0), (4, 4), (4, 4)))


def local(probe_field, bounds, courant, snapshots, snap_times, basis_panels):
    probes_here, depth_rows, cells_y, cells_z = probe_field.shape
    steps_total = snap_times.shape[0]
    all_snaps = lax.all_gather(snapshots, "probe", axis=2, tiled=True)
    row_start = lax.axis_index("store") * depth_rows
    inside = slab_mask(row_start + jnp.arange(depth_rows, dtype=jnp.int32), bounds)
    perturb = probe_field.astype(jnp.float32) * inside[:, :, None, None]
    earlier = jnp.zeros((probes_here, depth_rows, cells_y, cells_z), jnp.float32)
    current = earlier
    for turn_index in range(steps_total):
        picked = lax.dynamic_index_in_dim(all_snaps, snap_times[turn_index], 0, keepdims=False)
        padded = extended(current, (("store", 1),), 4)
        advanced = (
            2.0 * current
            - earlier
            + courant * laplace(side_frame(padded))
            + perturb * picked.astype(jnp.float32)
        )
        earlier = current
        current = advanced
    response_low = current.astype(jnp.bfloat16)
    flat_fields = response_low.reshape(probes_here, -1)
    portion = lax.all_gather(basis_panels, "probe", axis=0, tiled=True)
    product = lax.dot_general(
        portion.reshape(portion.shape[0], -1),
        flat_fields,
        (((1,), (1,)), ((), ())),
        preferred_element_type=jnp.float32,
    )
    projection = lax.psum(product, "store")
    return (current, projection)


def solution(mesh):
    placed = (
        P("probe", "store", None, None),
        P("probe", None),
        P("store", None, None),
        P(None, "store", "probe", None),
        P(),
        P("probe", "store", None, None),
    )
    return jax.shard_map(
        local,
        mesh=mesh,
        in_specs=placed,
        out_specs=(P("probe", "store", None, None), P(None, "probe")),
        check_vma=False,
    )
```

profile of v0, /device:TPU:0, one launch (start us, length us, event | category | flops | bytes accessed | tf_op | source)
XLA Modules:
  0.0 564.6 jit_solution(12925683046278286328)
XLA Ops:
  8.6 5.5 collective-permute-start.1
  14.1 1.6 fusion.274
  26.5 6.3 %all_gather.6 = bf16[8,16,8,128]{3,1,0,2:T(8,128)(2,1)S(1)} all-gather(bf16[8,16,2,128]{3,1,0,2:T(8,128)(2,1)S(1)} %copy.10), channel_id=1, replica_groups=mesh['probe'=4,'store'=8] {'probe'}, dimensions={2}, use_global_device_ids=true | all-gather | bytes 327680 | tf_op jit(solution)/shard_map/all_gather | solution.py:69
  39.8 4.0 fusion.231
  43.8 1.3 collective-permute-start.2
  45.1 4.9 collective-permute-start.3
  50.1 7.6 %collective-permute-done.2 = f32[24,4,8,128]{3,2,1,0:T(8,128)S(1)} collective-permute-done((f32[24,4,8,128]{3,2,1,0:T(8,128)S(1)}, f32[24,4,8,128]{3,2,1,0:T(8,128)S(1)}, u32[]{:S(2)}, u32[]{:S(2)}) %collective-permute-start.2) | collective-permute-done | bytes 393248 | tf_op jit(solution)/shard_map/ppermute | solution.py:17
  57.7 8.6 %collective-permute-done.3 = f32[24,4,8,128]{3,2,1,0:T(8,128)S(1)} collective-permute-done((f32[24,4,8,128]{3,2,1,0:T(8,128)S(1)}, f32[24,4,8,128]{3,2,1,0:T(8,128)S(1)}, u32[]{:S(2)}, u32[]{:S(2)}) %collective-permute-start.3) | collective-permute-done | bytes 393248 | tf_op jit(solution)/shard_map/ppermute | solution.py:16
  66.3 6.0 %select_maximum_fusion.12 = f32[24,24,16,136]{3,2,1,0:T(8,128)} fusion(f32[24,4,8,128]{3,2,1,0:T(8,128)S(1)} %collective-permute-done.2, f32[24,16,8,128]{3,2,1,0:T(8,128)S(1)} %fusion.231, f32[24,4,8,128]{3,2,1,0:T(8,128)S(1)} %collective-permute-done.3), kind=kLoop, calls=%fused_computation.32 | loop fusion | flops 18800640 | bytes 7372800 | tf_op jit(solution)/shard_map/concatenate | solution.py:18
  72.3 39.5 %fusion.200 = f32[24,16,8,128]{3,2,1,0:T(8,128)S(1)} fusion(f32[24,16,8,128]{3,2,1,0:T(8,128)} %copy-done.5, f32[24,4,8,128]{3,2,1,0:T(8,128)S(1)} %collective-permute-done.3, f32[24,4,8,128]{3,2,1,0:T(8,128)S(1)} %collective-permute-done.2, f32[24,24,16,136]{3,2,1,0:T(8,128)} %select_maximum_fusion.12, bf16[24,16,8,128]{3,2,1,0:T(8,128)(2,1)S(1)} %copy-done, ...), kind=kLoop, calls=%fused_computation.327 | loop fusion | flops 17301504 | bytes 30017024 | tf_op jit(solution)/shard_map/add | solution.py:79
  112.0 1.4 collective-permute-start.4
  113.4 5.0 collective-permute-start.5
  118.4 7.3 %collective-permute-done.4 = f32[24,4,8,128]{3,2,1,0:T(8,128)S(1)} collective-permute-done((f32[24,4,8,128]{3,2,1,0:T(8,128)S(1)}, f32[24,4,8,128]{3,2,1,0:T(8,128)S(1)}, u32[]{:S(2)}, u32[]{:S(2)}) %collective-permute-start.4) | collective-permute-done | bytes 393248 | tf_op jit(solution)/shard_map/ppermute | solution.py:17
  125.8 8.6 %collective-permute-done.5 = f32[24,4,8,128]{3,2,1,0:T(8,128)S(1)} collective-permute-done((f32[24,4,8,128]{3,2,1,0:T(8,128)S(1)}, f32[24,4,8,128]{3,2,1,0:T(8,128)S(1)}, u32[]{:S(2)}, u32[]{:S(2)}) %collective-permute-start.5) | collective-permute-done | bytes 393248 | tf_op jit(solution)/shard_map/ppermute | solution.py:16
  134.4 6.0 %select_maximum_fusion.10 = f32[24,24,16,136]{3,2,1,0:T(8,128)} fusion(f32[24,4,8,128]{3,2,1,0:T(8,128)S(1)} %collective-permute-done.4, f32[24,16,8,128]{3,2,1,0:T(8,128)S(1)} %fusion.200, f32[24,4,8,128]{3,2,1,0:T(8,128)S(1)} %collective-permute-done.5), kind=kLoop, calls=%fused_computation.30 | loop fusion | flops 18800640 | bytes 7372800 | tf_op jit(solution)/shard_map/concatenate | solution.py:18
  140.3 40.2 %fusion.169 = f32[24,16,8,128]{3,2,1,0:T(8,128)S(1)} fusion(f32[24,16,8,128]{3,2,1,0:T(8,128)} %copy-done.4, f32[24,4,8,128]{3,2,1,0:T(8,128)S(1)} %collective-permute-done.5, f32[24,4,8,128]{3,2,1,0:T(8,128)S(1)} %collective-permute-done.4, f32[24,24,16,136]{3,2,1,0:T(8,128)} %select_maximum_fusion.10, f32[24,16,8,128]{3,2,1,0:T(8,128)} %copy-done.5, ...), kind=kLoop, calls=%fused_computation.296 | loop fusion | flops 17694720 | bytes 31589888 | tf_op jit(solution)/shard_map/add | solution.py:79
  180.6 1.4 collective-permute-start.6
  182.0 5.2 collective-permute-start.7
  187.3 7.1 %collective-permute-done.6 = f32[24,4,8,128]{3,2,1,0:T(8,128)S(1)} collective-permute-done((f32[24,4,8,128]{3,2,1,0:T(8,128)S(1)}, f32[24,4,8,128]{3,2,1,0:T(8,128)S(1)}, u32[]{:S(2)}, u32[]{:S(2)}) %collective-permute-start.6) | collective-permute-done | bytes 393248 | tf_op jit(solution)/shard_map/ppermute | solution.py:17
  194.4 8.6 %collective-permute-done.7 = f32[24,4,8,128]{3,2,1,0:T(8,128)S(1)} collective-permute-done((f32[24,4,8,128]{3,2,1,0:T(8,128)S(1)}, f32[24,4,8,128]{3,2,1,0:T(8,128)S(1)}, u32[]{:S(2)}, u32[]{:S(2)}) %collective-permute-start.7) | collective-permute-done | bytes 393248 | tf_op jit(solution)/shard_map/ppermute | solution.py:16
  203.0 6.0 %select_maximum_fusion.8 = f32[24,24,16,136]{3,2,1,0:T(8,128)} fusion(f32[24,4,8,128]{3,2,1,0:T(8,128)S(1)} %collective-permute-done.6, f32[24,16,8,128]{3,2,1,0:T(8,128)S(1)} %fusion.169, f32[24,4,8,128]{3,2,1,0:T(8,128)S(1)} %collective-permute-done.7), kind=kLoop, calls=%fused_computation.28 | loop fusion | flops 18800640 | bytes 7372800 | tf_op jit(solution)/shard_map/concatenate | solution.py:18
  208.9 36.7 %fusion.138 = f32[24,16,8,128]{3,2,1,0:T(8,128)} fusion(f32[24,16,8,128]{3,2,1,0:T(8,128)S(1)} %fusion.169, f32[24,4,8,128]{3,2,1,0:T(8,128)S(1)} %collective-permute-done.7, f32[24,4,8,128]{3,2,1,0:T(8,128)S(1)} %collective-permute-done.6, f32[24,24,16,136]{3,2,1,0:T(8,128)} %select_maximum_fusion.8, f32[24,16,8,128]{3,2,1,0:T(8,128)} %copy-done.4, ...), kind=kLoop, calls=%fused_computation.265 | loop fusion | flops 17694720 | bytes 31589888 | tf_op jit(solution)/shard_map/add | solution.py:79
  245.7 1.3 fusion.270
  248.2 5.0 collective-permute-start.9
  253.3 7.3 %collective-permute-done.8 = f32[24,4,8,128]{3,2,1,0:T(8,128)S(1)} collective-permute-done((f32[24,4,8,128]{3,2,1,0:T(8,128)S(1)}, f32[24,4,8,128]{3,2,1,0:T(8,128)S(1)}, u32[]{:S(2)}, u32[]{:S(2)}) %collective-permute-start.8) | collective-permute-done | bytes 393248 | tf_op jit(solution)/shard_map/ppermute | solution.py:17
  260.6 8.6 %collective-permute-done.9 = f32[24,4,8,128]{3,2,1,0:T(8,128)S(1)} collective-permute-done((f32[24,4,8,128]{3,2,1,0:T(8,128)S(1)}, f32[24,4,8,128]{3,2,1,0:T(8,128)S(1)}, u32[]{:S(2)}, u32[]{:S(2)}) %collective-permute-start.9) | collective-permute-done | bytes 393248 | tf_op jit(solution)/shard_map/ppermute | solution.py:16
  269.2 6.0 %select_maximum_fusion.6 = f32[24,24,16,136]{3,2,1,0:T(8,128)} fusion(f32[24,4,8,128]{3,2,1,0:T(8,128)S(1)} %collective-permute-done.8, f32[24,16,8,128]{3,2,1,0:T(8,128)S(1)} %copy-done.3, f32[24,4,8,128]{3,2,1,0:T(8,128)S(1)} %collective-permute-done.9), kind=kLoop, calls=%fused_computation.26 | loop fusion | flops 18800640 | bytes 7372800 | tf_op jit(solution)/shard_map/concatenate | solution.py:18
  275.2 39.8 %fusion.107 = f32[24,16,8,128]{3,2,1,0:T(8,128)S(1)} fusion(f32[24,16,8,128]{3,2,1,0:T(8,128)} %fusion.138, f32[24,4,8,128]{3,2,1,0:T(8,128)S(1)} %collective-permute-done.9, f32[24,4,8,128]{3,2,1,0:T(8,128)S(1)} %collective-permute-done.8, f32[24,24,16,136]{3,2,1,0:T(8,128)} %select_maximum_fusion.6, f32[24,16,8,128]{3,2,1,0:T(8,128)} %copy-done.2, ...), kind=kLoop, calls=%fused_computation.234 | loop fusion | flops 17694720 | bytes 31589888 | tf_op jit(solution)/shard_map/add | solution.py:79
  315.1 1.3 collective-permute-start.10
  316.4 5.0 collective-permute-start.11
  321.5 7.3 %collective-permute-done.10 = f32[24,4,8,128]{3,2,1,0:T(8,128)S(1)} collective-permute-done((f32[24,4,8,128]{3,2,1,0:T(8,128)S(1)}, f32[24,4,8,128]{3,2,1,0:T(8,128)S(1)}, u32[]{:S(2)}, u32[]{:S(2)}) %collective-permute-start.10) | collective-permute-done | bytes 393248 | tf_op jit(solution)/shard_map/ppermute | solution.py:17
  328.8 8.6 %collective-permute-done.11 = f32[24,4,8,128]{3,2,1,0:T(8,128)S(1)} collective-permute-done((f32[24,4,8,128]{3,2,1,0:T(8,128)S(1)}, f32[24,4,8,128]{3,2,1,0:T(8,128)S(1)}, u32[]{:S(2)}, u32[]{:S(2)}) %collective-permute-start.11) | collective-permute-done | bytes 393248 | tf_op jit(solution)/shard_map/ppermute | solution.py:16
  337.4 6.0 %select_maximum_fusion.4 = f32[24,24,16,136]{3,2,1,0:T(8,128)} fusion(f32[24,4,8,128]{3,2,1,0:T(8,128)S(1)} %collective-permute-done.10, f32[24,16,8,128]{3,2,1,0:T(8,128)S(1)} %fusion.107, f32[24,4,8,128]{3,2,1,0:T(8,128)S(1)} %collective-permute-done.11), kind=kLoop, calls=%fused_computation.24 | loop fusion | flops 18800640 | bytes 7372800 | tf_op jit(solution)/shard_map/concatenate | solution.py:18
  343.3 39.2 %fusion.76 = f32[24,16,8,128]{3,2,1,0:T(8,128)S(1)} fusion(f32[24,16,8,128]{3,2,1,0:T(8,128)} %copy-done.1, f32[24,4,8,128]{3,2,1,0:T(8,128)S(1)} %collective-permute-done.11, f32[24,4,8,128]{3,2,1,0:T(8,128)S(1)} %collective-permute-done.10, f32[24,24,16,136]{3,2,1,0:T(8,128)} %select_maximum_fusion.4, f32[24,16,8,128]{3,2,1,0:T(8,128)} %fusion.138, ...), kind=kLoop, calls=%fused_computation.203 | loop fusion | flops 17694720 | bytes 31589888 | tf_op jit(solution)/shard_map/add | solution.py:79
  384.8 5.3 collective-permute-start.13
  390.1 1.4 copy.19
  391.5 5.9 %collective-permute-done.12 = f32[24,4,8,128]{3,2,1,0:T(8,128)S(1)} collective-permute-done((f32[24,4,8,128]{3,2,1,0:T(8,128)}, f32[24,4,8,128]{3,2,1,0:T(8,128)S(1)}, u32[]{:S(2)}, u32[]{:S(2)}) %collective-permute-start.12) | collective-permute-done | bytes 393248 | tf_op jit(solution)/shard_map/ppermute | solution.py:17
  397.4 8.7 %collective-permute-done.13 = f32[24,4,8,128]{3,2,1,0:T(8,128)S(1)} collective-permute-done((f32[24,4,8,128]{3,2,1,0:T(8,128)}, f32[24,4,8,128]{3,2,1,0:T(8,128)S(1)}, u32[]{:S(2)}, u32[]{:S(2)}) %collective-permute-start.13) | collective-permute-done | bytes 393248 | tf_op jit(solution)/shard_map/ppermute | solution.py:16
  406.1 6.0 %select_maximum_fusion.2 = f32[24,24,16,136]{3,2,1,0:T(8,128)} fusion(f32[24,4,8,128]{3,2,1,0:T(8,128)S(1)} %collective-permute-done.12, f32[24,16,8,128]{3,2,1,0:T(8,128)S(1)} %fusion.76, f32[24,4,8,128]{3,2,1,0:T(8,128)S(1)} %collective-permute-done.13), kind=kLoop, calls=%fused_computation.22 | loop fusion | flops 18800640 | bytes 7372800 | tf_op jit(solution)/shard_map/concatenate | solution.py:18
  412.0 36.5 %fusion.45 = f32[24,16,8,128]{3,2,1,0:T(8,128)} fusion(f32[24,16,8,128]{3,2,1,0:T(8,128)S(1)} %fusion.76, f32[24,4,8,128]{3,2,1,0:T(8,128)S(1)} %collective-permute-done.13, f32[24,4,8,128]{3,2,1,0:T(8,128)S(1)} %collective-permute-done.12, f32[24,24,16,136]{3,2,1,0:T(8,128)} %select_maximum_fusion.2, f32[24,16,8,128]{3,2,1,0:T(8,128)} %copy-done.1, ...), kind=kLoop, calls=%fused_computation.172 | loop fusion | flops 17694720 | bytes 31589888 | tf_op jit(solution)/shard_map/add | solution.py:79
  448.5 1.3 fusion.267
  451.1 4.9 collective-permute-start.15
  456.1 7.4 %collective-permute-done.14 = f32[24,4,8,128]{3,2,1,0:T(8,128)S(1)} collective-permute-done((f32[24,4,8,128]{3,2,1,0:T(8,128)S(1)}, f32[24,4,8,128]{3,2,1,0:T(8,128)S(1)}, u32[]{:S(2)}, u32[]{:S(2)}) %collective-permute-start.14) | collective-permute-done | bytes 393248 | tf_op jit(solution)/shard_map/ppermute | solution.py:17
  463.5 8.6 %collective-permute-done.15 = f32[24,4,8,128]{3,2,1,0:T(8,128)S(1)} collective-permute-done((f32[24,4,8,128]{3,2,1,0:T(8,128)S(1)}, f32[24,4,8,128]{3,2,1,0:T(8,128)S(1)}, u32[]{:S(2)}, u32[]{:S(2)}) %collective-permute-start.15) | collective-permute-done | bytes 393248 | tf_op jit(solution)/shard_map/ppermute | solution.py:16
  472.8 6.0 %select_maximum_fusion = f32[24,24,16,136]{3,2,1,0:T(8,128)} fusion(f32[24,4,8,128]{3,2,1,0:T(8,128)S(1)} %collective-permute-done.14, f32[24,16,8,128]{3,2,1,0:T(8,128)S(1)} %copy-done.6, f32[24,4,8,128]{3,2,1,0:T(8,128)S(1)} %collective-permute-done.15), kind=kLoop, calls=%fused_computation.20 | loop fusion | flops 18800640 | bytes 7372800 | tf_op jit(solution)/shard_map/concatenate | solution.py:18
  478.8 40.4 %fusion.265 = (bf16[24,16,8,128]{3,2,1,0:T(8,128)(2,1)S(1)}, f32[24,16,8,128]{3,2,1,0:T(8,128)}) fusion(f32[16,8,128]{2,1,0:T(8,128)S(1)} %copy.18, f32[24,16]{1,0:T(8,128)S(1)} %and_convert_fusion, bf16[24,16,8,128]{3,2,1,0:T(8,128)(2,1)S(1)} %copy-done, f32[24,24,16,136]{3,2,1,0:T(8,128)} %select_maximum_fusion, f32[24,16,8,128]{3,2,1,0:T(8,128)} %fusion.45, ...), kind=kLoop, calls=%fused_computation.448 | loop fusion | flops 18087936 | bytes 32376320 | tf_op jit(solution)/shard_map/convert_element_type | solution.py:86
  519.2 3.0 convolution_bitcast_fusion
  522.2 35.5 %psum.7 = f32[96,24]{0,1:T(8,128)} all-reduce(f32[96,24]{0,1:T(8,128)S(1)} %convolution_bitcast_fusion), channel_id=1, replica_groups=mesh['probe'=4,'store'=8] {'store'}, use_global_device_ids=true, to_apply=%region_0.1 | all-reduce | flops 2304 | bytes 18432 | tf_op jit(solution)/shard_map/psum | solution.py:95
  (59 shorter events, 10.3 us)
Async XLA Ops:
  7.2 31.4 %copy-start.13 = (s32[24,2]{0,1:T(2,128)S(1)}, s32[24,2]{0,1:T(2,128)}, u32[]{:S(2)}) copy-start(s32[24,2]{0,1:T(2,128)} %param.7) | copy-start | bytes 580
  7.2 512.0 %all-gather.2.cloned.1.call-start = ((), (), s32[]{:S(2)}) async-start(), calls=%async_computation | async-start | bytes 3932160 | tf_op jit(solution)/shard_map/all_gather | solution.py:88
  7.3 31.4 %collective-permute-start = (f32[24,4,8,128]{3,2,1,0:T(8,128)S(1)}, f32[24,4,8,128]{3,2,1,0:T(8,128)S(1)}, u32[]{:S(2)}, u32[]{:S(2)}) collective-permute-start(f32[24,4,8,128]{3,2,1,0:T(8,128)S(1)} %broadcast.90), channel_id=1, source_target_pairs={{1,0},{2,1},{3,2},{4,3},{5,4},{6,5},{7,6},{9,8},{10,9},{11,10},{12... | collective-permute-start | bytes 1179656 | tf_op jit(solution)/shard_map/ppermute | solution.py:17
  8.6 30.1 %collective-permute-start.1 = (f32[24,4,8,128]{3,2,1,0:T(8,128)S(1)}, f32[24,4,8,128]{3,2,1,0:T(8,128)S(1)}, u32[]{:S(2)}, u32[]{:S(2)}) collective-permute-start(f32[24,4,8,128]{3,2,1,0:T(8,128)S(1)} %broadcast.90), channel_id=1, source_target_pairs={{0,1},{1,2},{2,3},{3,4},{4,5},{5,6},{6,7},{8,9},{9,10},{10,11},{11... | collective-permute-start | bytes 1179656 | tf_op jit(solution)/shard_map/ppermute | solution.py:16
  38.7 1.1 copy-start
  38.7 1.1 copy-start.7
  43.8 22.6 %copy-start.5 = (f32[24,16,8,128]{3,2,1,0:T(8,128)}, f32[24,16,8,128]{3,2,1,0:T(8,128)S(1)}, u32[]{:S(2)}) copy-start(f32[24,16,8,128]{3,2,1,0:T(8,128)S(1)} %fusion.231) | copy-start | bytes 4718596
  43.8 13.9 %collective-permute-start.2 = (f32[24,4,8,128]{3,2,1,0:T(8,128)S(1)}, f32[24,4,8,128]{3,2,1,0:T(8,128)S(1)}, u32[]{:S(2)}, u32[]{:S(2)}) collective-permute-start(f32[24,4,8,128]{3,2,1,0:T(8,128)S(1)} %get-tuple-element.16), channel_id=1, source_target_pairs={{1,0},{2,1},{3,2},{4,3},{5,4},{6,5},{7,6},{9,8},{10,9},{11,10},{12... | collective-permute-start | bytes 1179656 | tf_op jit(solution)/shard_map/ppermute | solution.py:17
  45.1 21.2 %collective-permute-start.3 = (f32[24,4,8,128]{3,2,1,0:T(8,128)S(1)}, f32[24,4,8,128]{3,2,1,0:T(8,128)S(1)}, u32[]{:S(2)}, u32[]{:S(2)}) collective-permute-start(f32[24,4,8,128]{3,2,1,0:T(8,128)S(1)} %get-tuple-element.17), channel_id=1, source_target_pairs={{0,1},{1,2},{2,3},{3,4},{4,5},{5,6},{6,7},{8,9},{9,10},{10,11},{11... | collective-permute-start | bytes 1179656 | tf_op jit(solution)/shard_map/ppermute | solution.py:16
  111.9 22.5 %copy-start.4 = (f32[24,16,8,128]{3,2,1,0:T(8,128)}, f32[24,16,8,128]{3,2,1,0:T(8,128)S(1)}, u32[]{:S(2)}) copy-start(f32[24,16,8,128]{3,2,1,0:T(8,128)S(1)} %fusion.200) | copy-start | bytes 4718596
  111.9 6.5 %copy-start.12 = (f32[16,8,128]{2,0,1:T(8,128)S(1)}, f32[16,8,128]{2,0,1:T(8,128)}, u32[]{:S(2)}) copy-start(f32[16,8,128]{2,0,1:T(8,128)} %get-tuple-element.23) | copy-start | bytes 196612
  112.0 13.8 %collective-permute-start.4 = (f32[24,4,8,128]{3,2,1,0:T(8,128)S(1)}, f32[24,4,8,128]{3,2,1,0:T(8,128)S(1)}, u32[]{:S(2)}, u32[]{:S(2)}) collective-permute-start(f32[24,4,8,128]{3,2,1,0:T(8,128)S(1)} %get-tuple-element.14), channel_id=1, source_target_pairs={{1,0},{2,1},{3,2},{4,3},{5,4},{6,5},{7,6},{9,8},{10,9},{11,10},{12... | collective-permute-start | bytes 1179656 | tf_op jit(solution)/shard_map/ppermute | solution.py:17
  113.4 21.0 %collective-permute-start.5 = (f32[24,4,8,128]{3,2,1,0:T(8,128)S(1)}, f32[24,4,8,128]{3,2,1,0:T(8,128)S(1)}, u32[]{:S(2)}, u32[]{:S(2)}) collective-permute-start(f32[24,4,8,128]{3,2,1,0:T(8,128)S(1)} %get-tuple-element.15), channel_id=1, source_target_pairs={{0,1},{1,2},{2,3},{3,4},{4,5},{5,6},{6,7},{8,9},{9,10},{10,11},{11... | collective-permute-start | bytes 1179656 | tf_op jit(solution)/shard_map/ppermute | solution.py:16
  180.5 28.5 %copy-start.2 = (f32[24,16,8,128]{3,2,1,0:T(8,128)}, f32[24,16,8,128]{3,2,1,0:T(8,128)S(1)}, u32[]{:S(2)}) copy-start(f32[24,16,8,128]{3,2,1,0:T(8,128)S(1)} %fusion.169) | copy-start | bytes 4718596
  180.5 6.7 %copy-start.11 = (f32[16,8,128]{2,0,1:T(8,128)S(1)}, f32[16,8,128]{2,0,1:T(8,128)}, u32[]{:S(2)}) copy-start(f32[16,8,128]{2,0,1:T(8,128)} %get-tuple-element.22) | copy-start | bytes 196612
  180.6 13.8 %collective-permute-start.6 = (f32[24,4,8,128]{3,2,1,0:T(8,128)S(1)}, f32[24,4,8,128]{3,2,1,0:T(8,128)S(1)}, u32[]{:S(2)}, u32[]{:S(2)}) collective-permute-start(f32[24,4,8,128]{3,2,1,0:T(8,128)S(1)} %get-tuple-element.12), channel_id=1, source_target_pairs={{1,0},{2,1},{3,2},{4,3},{5,4},{6,5},{7,6},{9,8},{10,9},{11,10},{12... | collective-permute-start | bytes 1179656 | tf_op jit(solution)/shard_map/ppermute | solution.py:17
  182.0 21.0 %collective-permute-start.7 = (f32[24,4,8,128]{3,2,1,0:T(8,128)S(1)}, f32[24,4,8,128]{3,2,1,0:T(8,128)S(1)}, u32[]{:S(2)}, u32[]{:S(2)}) collective-permute-start(f32[24,4,8,128]{3,2,1,0:T(8,128)S(1)} %get-tuple-element.13), channel_id=1, source_target_pairs={{0,1},{1,2},{2,3},{3,4},{4,5},{5,6},{6,7},{8,9},{9,10},{10,11},{11... | collective-permute-start | bytes 1179656 | tf_op jit(solution)/shard_map/ppermute | solution.py:16
  245.6 23.6 %copy-start.3 = (f32[24,16,8,128]{3,2,1,0:T(8,128)S(1)}, f32[24,16,8,128]{3,2,1,0:T(8,128)}, u32[]{:S(2)}) copy-start(f32[24,16,8,128]{3,2,1,0:T(8,128)} %fusion.138) | copy-start | bytes 4718596
  246.9 13.7 %collective-permute-start.8 = (f32[24,4,8,128]{3,2,1,0:T(8,128)S(1)}, f32[24,4,8,128]{3,2,1,0:T(8,128)S(1)}, u32[]{:S(2)}, u32[]{:S(2)}) collective-permute-start(f32[24,4,8,128]{3,2,1,0:T(8,128)S(1)} %get-tuple-element.10), channel_id=1, source_target_pairs={{1,0},{2,1},{3,2},{4,3},{5,4},{6,5},{7,6},{9,8},{10,9},{11,10},{12... | collective-permute-start | bytes 1179656 | tf_op jit(solution)/shard_map/ppermute | solution.py:17
  248.2 21.0 %collective-permute-start.9 = (f32[24,4,8,128]{3,2,1,0:T(8,128)S(1)}, f32[24,4,8,128]{3,2,1,0:T(8,128)S(1)}, u32[]{:S(2)}, u32[]{:S(2)}) collective-permute-start(f32[24,4,8,128]{3,2,1,0:T(8,128)S(1)} %get-tuple-element.11), channel_id=1, source_target_pairs={{0,1},{1,2},{2,3},{3,4},{4,5},{5,6},{6,7},{8,9},{9,10},{10,11},{11... | collective-permute-start | bytes 1179656 | tf_op jit(solution)/shard_map/ppermute | solution.py:16
  315.0 22.3 %copy-start.1 = (f32[24,16,8,128]{3,2,1,0:T(8,128)}, f32[24,16,8,128]{3,2,1,0:T(8,128)S(1)}, u32[]{:S(2)}) copy-start(f32[24,16,8,128]{3,2,1,0:T(8,128)S(1)} %fusion.107) | copy-start | bytes 4718596
  315.1 13.7 %collective-permute-start.10 = (f32[24,4,8,128]{3,2,1,0:T(8,128)S(1)}, f32[24,4,8,128]{3,2,1,0:T(8,128)S(1)}, u32[]{:S(2)}, u32[]{:S(2)}) collective-permute-start(f32[24,4,8,128]{3,2,1,0:T(8,128)S(1)} %get-tuple-element.8), channel_id=1, source_target_pairs={{1,0},{2,1},{3,2},{4,3},{5,4},{6,5},{7,6},{9,8},{10,9},{11,10},{12... | collective-permute-start | bytes 1179656 | tf_op jit(solution)/shard_map/ppermute | solution.py:17
  316.4 21.0 %collective-permute-start.11 = (f32[24,4,8,128]{3,2,1,0:T(8,128)S(1)}, f32[24,4,8,128]{3,2,1,0:T(8,128)S(1)}, u32[]{:S(2)}, u32[]{:S(2)}) collective-permute-start(f32[24,4,8,128]{3,2,1,0:T(8,128)S(1)} %get-tuple-element.9), channel_id=1, source_target_pairs={{0,1},{1,2},{2,3},{3,4},{4,5},{5,6},{6,7},{8,9},{9,10},{10,11},{11... | collective-permute-start | bytes 1179656 | tf_op jit(solution)/shard_map/ppermute | solution.py:16
  382.5 7.5 %copy-start.10 = (bf16[24,16,8,128]{3,2,1,0:T(8,128)(2,1)S(1)}, bf16[24,16,8,128]{3,2,1,0:T(8,128)(2,1)}, u32[]{:S(2)}) copy-start(bf16[24,16,8,128]{3,2,1,0:T(8,128)(2,1)} %param.11) | copy-start | bytes 2359300
  383.5 13.9 %collective-permute-start.12 = (f32[24,4,8,128]{3,2,1,0:T(8,128)}, f32[24,4,8,128]{3,2,1,0:T(8,128)S(1)}, u32[]{:S(2)}, u32[]{:S(2)}) collective-permute-start(f32[24,4,8,128]{3,2,1,0:T(8,128)} %get-tuple-element.6), channel_id=1, source_target_pairs={{1,0},{2,1},{3,2},{4,3},{5,4},{6,5},{7,6},{9,8},{10,9},{11,10},{12... | collective-permute-start | bytes 1179656 | tf_op jit(solution)/shard_map/ppermute | solution.py:17
  384.8 21.3 %collective-permute-start.13 = (f32[24,4,8,128]{3,2,1,0:T(8,128)}, f32[24,4,8,128]{3,2,1,0:T(8,128)S(1)}, u32[]{:S(2)}, u32[]{:S(2)}) collective-permute-start(f32[24,4,8,128]{3,2,1,0:T(8,128)} %get-tuple-element.7), channel_id=1, source_target_pairs={{0,1},{1,2},{2,3},{3,4},{4,5},{5,6},{6,7},{8,9},{9,10},{10,11},{11... | collective-permute-start | bytes 1179656 | tf_op jit(solution)/shard_map/ppermute | solution.py:16
  448.5 24.3 %copy-start.6 = (f32[24,16,8,128]{3,2,1,0:T(8,128)S(1)}, f32[24,16,8,128]{3,2,1,0:T(8,128)}, u32[]{:S(2)}) copy-start(f32[24,16,8,128]{3,2,1,0:T(8,128)} %fusion.45) | copy-start | bytes 4718596
  449.8 13.7 %collective-permute-start.14 = (f32[24,4,8,128]{3,2,1,0:T(8,128)S(1)}, f32[24,4,8,128]{3,2,1,0:T(8,128)S(1)}, u32[]{:S(2)}, u32[]{:S(2)}) collective-permute-start(f32[24,4,8,128]{3,2,1,0:T(8,128)S(1)} %get-tuple-element.5), channel_id=1, source_target_pairs={{1,0},{2,1},{3,2},{4,3},{5,4},{6,5},{7,6},{9,8},{10,9},{11,10},{12... | collective-permute-start | bytes 1179656 | tf_op jit(solution)/shard_map/ppermute | solution.py:17
  451.1 21.0 %collective-permute-start.15 = (f32[24,4,8,128]{3,2,1,0:T(8,128)S(1)}, f32[24,4,8,128]{3,2,1,0:T(8,128)S(1)}, u32[]{:S(2)}, u32[]{:S(2)}) collective-permute-start(f32[24,4,8,128]{3,2,1,0:T(8,128)S(1)} %get-tuple-element.4), channel_id=1, source_target_pairs={{0,1},{1,2},{2,3},{3,4},{4,5},{5,6},{6,7},{8,9},{9,10},{10,11},{11... | collective-permute-start | bytes 1179656 | tf_op jit(solution)/shard_map/ppermute | solution.py:16
  463.5 8.6 %copy-start.8 = (f32[24,4,8,128]{3,2,1,0:T(8,128)}, f32[24,4,8,128]{3,2,1,0:T(8,128)S(1)}, u32[]{:S(2)}) copy-start(f32[24,4,8,128]{3,2,1,0:T(8,128)S(1)} %collective-permute-done.14) | copy-start | bytes 1179652
  472.1 0.8 copy-start.9
Sparse Core Ops, SparseCore 0:
  391.6 30.1 all-gather.1
where the time goes:
time: 566 us; the launch traced here: 565 us
  other arithmetic  319 us (56%)
  waiting for transfers between devices  110 us (19%)
  starting transfers between devices  51.6 us (9%)
  blocking collectives  41.8 us (7%)
  between operations  29.4 us (5%)
  local copies, waits for them, and re-layouts  9.52 us (2%)
    add x7, other arithmetic, local(): 2.0 * current - earlier + courant * laplace(side_frame(padded))  236 us
    ppermute x8, waiting for transfers between devices, extended(): before = lax.ppermute(last, axis, up)  60.2 us
    ppermute x8, waiting for transfers between devices, extended(): after = lax.ppermute(leading, axis, down)  50 us
    concatenate x8, other arithmetic, extended(): x = jnp.concatenate([before, x, after], axis=dim)  42.1 us
    ppermute x8, starting transfers between devices, extended(): before = lax.ppermute(last, axis, up)  40.9 us
    convert_element_type x1, other arithmetic, local(): response_low = current.astype(jnp.bfloat16)  40.4 us
    psum x1, blocking collectives, local(): projection = lax.psum(product, 'store')  35.5 us
  transfers between devices with their start and end apart: 17, of which 14 were waited for; matrix products, arithmetic and copies ran while one was open for 17% of the time, Pallas kernels for 0%

commit v1 on v0

--- a/solution.py
+++ b/solution.py
@@ -92,7 +92,11 @@
         (((1,), (1,)), ((), ())),
         preferred_element_type=jnp.float32,
     )
-    projection = lax.psum(product, "store")
+    projection = product
+    for hop in (1, 2, 4):
+        projection = projection + lax.ppermute(
+            projection, "store", [(dev, dev ^ hop) for dev in range(8)]
+        )
     return (current, projection)
 
 

time: 566 us -> 549 us (0.970)
  blocking collectives: 41.8 us -> 6.3 us
  other arithmetic: 319 us -> 326 us
  starting transfers between devices: 51.6 us -> 58.5 us
  waiting for transfers between devices: 110 us -> 116 us
    psum x1 -> x0, blocking collectives: 35.5 us -> none  [local(): projection = lax.psum(product, 'store')]
    ppermute x0 -> x3, starting transfers between devices: none -> 6.9 us  [local(): lax.ppermute(projection, 'store', [(dev, dev ^ hop) for dev in range(8)])]
  transfers between devices with their start and end apart: 17 -> 20, of which waited for: 14 -> 17; matrix products, arithmetic and copies ran while one was open for 17% -> 18% of each run, Pallas kernels for 0% -> 0%
where the time goes in v1:
time: 549 us; the launch traced here: 548 us
  other arithmetic  326 us (59%)
  waiting for transfers between devices  116 us (21%)
  starting transfers between devices  58.5 us (11%)
  between operations  29.2 us (5%)
  local copies, waits for them, and re-layouts  9.53 us (2%)
  blocking collectives  6.3 us (1%)
    add x7, other arithmetic, local(): 2.0 * current - earlier + courant * laplace(side_frame(padded))  241 us
    ppermute x8, waiting for transfers between devices, extended(): before = lax.ppermute(last, axis, up)  60.2 us
    ppermute x8, waiting for transfers between devices, extended(): after = lax.ppermute(leading, axis, down)  49.9 us
    concatenate x8, other arithmetic, extended(): x = jnp.concatenate([before, x, after], axis=dim)  42.3 us
    convert_element_type x1, other arithmetic, local(): response_low = current.astype(jnp.bfloat16)  41.3 us
    ppermute x8, starting transfers between devices, extended(): before = lax.ppermute(last, axis, up)  40.9 us
  transfers between devices with their start and end apart: 20, of which 17 were waited for; matrix products, arithmetic and copies ran while one was open for 18% of the time, Pallas kernels for 0%

profile of v1, /device:TPU:0, one launch (start us, length us, event | category | flops | bytes accessed | tf_op | source)
XLA Modules:
  0.0 548.4 jit_solution(2628938198755227193)
XLA Ops:
  8.6 5.5 %collective-permute-start.1 = (f32[24,4,8,128]{3,2,1,0:T(8,128)S(1)}, f32[24,4,8,128]{3,2,1,0:T(8,128)S(1)}, u32[]{:S(2)}, u32[]{:S(2)}) collective-permute-start(f32[24,4,8,128]{3,2,1,0:T(8,128)S(1)} %broadcast.90), channel_id=1, source_target_pairs={{0,1},{1,2},{2,3},{3,4},{4,5},{5,6},{6,7},{8,9},{9,10},{10,11},{11... | collective-permute-start | bytes 1179656 | tf_op jit(solution)/shard_map/ppermute | solution.py:16
  14.1 1.6 fusion.274
  26.4 6.3 %all_gather.6 = bf16[8,16,8,128]{3,1,0,2:T(8,128)(2,1)S(1)} all-gather(bf16[8,16,2,128]{3,1,0,2:T(8,128)(2,1)S(1)} %copy.10), channel_id=1, replica_groups=mesh['probe'=4,'store'=8] {'probe'}, dimensions={2}, use_global_device_ids=true | all-gather | bytes 327680 | tf_op jit(solution)/shard_map/all_gather | solution.py:69
  39.6 4.0 fusion.231
  45.0 4.9 collective-permute-start.3
  50.0 7.6 %collective-permute-done.2 = f32[24,4,8,128]{3,2,1,0:T(8,128)S(1)} collective-permute-done((f32[24,4,8,128]{3,2,1,0:T(8,128)S(1)}, f32[24,4,8,128]{3,2,1,0:T(8,128)S(1)}, u32[]{:S(2)}, u32[]{:S(2)}) %collective-permute-start.2) | collective-permute-done | bytes 393248 | tf_op jit(solution)/shard_map/ppermute | solution.py:17
  57.6 8.6 %collective-permute-done.3 = f32[24,4,8,128]{3,2,1,0:T(8,128)S(1)} collective-permute-done((f32[24,4,8,128]{3,2,1,0:T(8,128)S(1)}, f32[24,4,8,128]{3,2,1,0:T(8,128)S(1)}, u32[]{:S(2)}, u32[]{:S(2)}) %collective-permute-start.3) | collective-permute-done | bytes 393248 | tf_op jit(solution)/shard_map/ppermute | solution.py:16
  66.2 6.0 %select_maximum_fusion.12 = f32[24,24,16,136]{3,2,1,0:T(8,128)} fusion(f32[24,4,8,128]{3,2,1,0:T(8,128)S(1)} %collective-permute-done.2, f32[24,16,8,128]{3,2,1,0:T(8,128)S(1)} %fusion.231, f32[24,4,8,128]{3,2,1,0:T(8,128)S(1)} %collective-permute-done.3), kind=kLoop, calls=%fused_computation.32 | loop fusion | flops 18800640 | bytes 7372800 | tf_op jit(solution)/shard_map/concatenate | solution.py:18
  72.2 40.5 %fusion.200 = f32[24,16,8,128]{3,2,1,0:T(8,128)S(1)} fusion(f32[24,16,8,128]{3,2,1,0:T(8,128)} %copy-done.5, f32[24,4,8,128]{3,2,1,0:T(8,128)S(1)} %collective-permute-done.3, f32[24,4,8,128]{3,2,1,0:T(8,128)S(1)} %collective-permute-done.2, f32[24,24,16,136]{3,2,1,0:T(8,128)} %select_maximum_fusion.12, bf16[24,16,8,128]{3,2,1,0:T(8,128)(2,1)S(1)} %copy-done, ...), kind=kLoop, calls=%fused_computation.327 | loop fusion | flops 17301504 | bytes 30017024 | tf_op jit(solution)/shard_map/add | solution.py:79
  112.8 1.4 collective-permute-start.4
  114.2 5.0 collective-permute-start.5
  119.3 7.3 %collective-permute-done.4 = f32[24,4,8,128]{3,2,1,0:T(8,128)S(1)} collective-permute-done((f32[24,4,8,128]{3,2,1,0:T(8,128)S(1)}, f32[24,4,8,128]{3,2,1,0:T(8,128)S(1)}, u32[]{:S(2)}, u32[]{:S(2)}) %collective-permute-start.4) | collective-permute-done | bytes 393248 | tf_op jit(solution)/shard_map/ppermute | solution.py:17
  126.6 8.6 %collective-permute-done.5 = f32[24,4,8,128]{3,2,1,0:T(8,128)S(1)} collective-permute-done((f32[24,4,8,128]{3,2,1,0:T(8,128)S(1)}, f32[24,4,8,128]{3,2,1,0:T(8,128)S(1)}, u32[]{:S(2)}, u32[]{:S(2)}) %collective-permute-start.5) | collective-permute-done | bytes 393248 | tf_op jit(solution)/shard_map/ppermute | solution.py:16
  135.2 6.0 %select_maximum_fusion.10 = f32[24,24,16,136]{3,2,1,0:T(8,128)} fusion(f32[24,4,8,128]{3,2,1,0:T(8,128)S(1)} %collective-permute-done.4, f32[24,16,8,128]{3,2,1,0:T(8,128)S(1)} %fusion.200, f32[24,4,8,128]{3,2,1,0:T(8,128)S(1)} %collective-permute-done.5), kind=kLoop, calls=%fused_computation.30 | loop fusion | flops 18800640 | bytes 7372800 | tf_op jit(solution)/shard_map/concatenate | solution.py:18
  141.2 41.1 %fusion.169 = f32[24,16,8,128]{3,2,1,0:T(8,128)S(1)} fusion(f32[24,16,8,128]{3,2,1,0:T(8,128)} %copy-done.4, f32[24,4,8,128]{3,2,1,0:T(8,128)S(1)} %collective-permute-done.5, f32[24,4,8,128]{3,2,1,0:T(8,128)S(1)} %collective-permute-done.4, f32[24,24,16,136]{3,2,1,0:T(8,128)} %select_maximum_fusion.10, f32[24,16,8,128]{3,2,1,0:T(8,128)} %copy-done.5, ...), kind=kLoop, calls=%fused_computation.296 | loop fusion | flops 17694720 | bytes 31589888 | tf_op jit(solution)/shard_map/add | solution.py:79
  182.4 1.4 collective-permute-start.6
  183.8 5.2 collective-permute-start.7
  189.1 7.1 %collective-permute-done.6 = f32[24,4,8,128]{3,2,1,0:T(8,128)S(1)} collective-permute-done((f32[24,4,8,128]{3,2,1,0:T(8,128)S(1)}, f32[24,4,8,128]{3,2,1,0:T(8,128)S(1)}, u32[]{:S(2)}, u32[]{:S(2)}) %collective-permute-start.6) | collective-permute-done | bytes 393248 | tf_op jit(solution)/shard_map/ppermute | solution.py:17
  196.2 8.6 %collective-permute-done.7 = f32[24,4,8,128]{3,2,1,0:T(8,128)S(1)} collective-permute-done((f32[24,4,8,128]{3,2,1,0:T(8,128)S(1)}, f32[24,4,8,128]{3,2,1,0:T(8,128)S(1)}, u32[]{:S(2)}, u32[]{:S(2)}) %collective-permute-start.7) | collective-permute-done | bytes 393248 | tf_op jit(solution)/shard_map/ppermute | solution.py:16
  204.8 6.0 %select_maximum_fusion.8 = f32[24,24,16,136]{3,2,1,0:T(8,128)} fusion(f32[24,4,8,128]{3,2,1,0:T(8,128)S(1)} %collective-permute-done.6, f32[24,16,8,128]{3,2,1,0:T(8,128)S(1)} %fusion.169, f32[24,4,8,128]{3,2,1,0:T(8,128)S(1)} %collective-permute-done.7), kind=kLoop, calls=%fused_computation.28 | loop fusion | flops 18800640 | bytes 7372800 | tf_op jit(solution)/shard_map/concatenate | solution.py:18
  210.7 37.7 %fusion.138 = f32[24,16,8,128]{3,2,1,0:T(8,128)} fusion(f32[24,16,8,128]{3,2,1,0:T(8,128)S(1)} %fusion.169, f32[24,4,8,128]{3,2,1,0:T(8,128)S(1)} %collective-permute-done.7, f32[24,4,8,128]{3,2,1,0:T(8,128)S(1)} %collective-permute-done.6, f32[24,24,16,136]{3,2,1,0:T(8,128)} %select_maximum_fusion.8, f32[24,16,8,128]{3,2,1,0:T(8,128)} %copy-done.4, ...), kind=kLoop, calls=%fused_computation.265 | loop fusion | flops 17694720 | bytes 31589888 | tf_op jit(solution)/shard_map/add | solution.py:79
  251.0 5.0 collective-permute-start.9
  256.1 7.3 %collective-permute-done.8 = f32[24,4,8,128]{3,2,1,0:T(8,128)S(1)} collective-permute-done((f32[24,4,8,128]{3,2,1,0:T(8,128)S(1)}, f32[24,4,8,128]{3,2,1,0:T(8,128)S(1)}, u32[]{:S(2)}, u32[]{:S(2)}) %collective-permute-start.8) | collective-permute-done | bytes 393248 | tf_op jit(solution)/shard_map/ppermute | solution.py:17
  263.4 8.6 %collective-permute-done.9 = f32[24,4,8,128]{3,2,1,0:T(8,128)S(1)} collective-permute-done((f32[24,4,8,128]{3,2,1,0:T(8,128)S(1)}, f32[24,4,8,128]{3,2,1,0:T(8,128)S(1)}, u32[]{:S(2)}, u32[]{:S(2)}) %collective-permute-start.9) | collective-permute-done | bytes 393248 | tf_op jit(solution)/shard_map/ppermute | solution.py:16
  272.0 6.0 %select_maximum_fusion.6 = f32[24,24,16,136]{3,2,1,0:T(8,128)} fusion(f32[24,4,8,128]{3,2,1,0:T(8,128)S(1)} %collective-permute-done.8, f32[24,16,8,128]{3,2,1,0:T(8,128)S(1)} %copy-done.3, f32[24,4,8,128]{3,2,1,0:T(8,128)S(1)} %collective-permute-done.9), kind=kLoop, calls=%fused_computation.26 | loop fusion | flops 18800640 | bytes 7372800 | tf_op jit(solution)/shard_map/concatenate | solution.py:18
  278.0 40.8 %fusion.107 = f32[24,16,8,128]{3,2,1,0:T(8,128)S(1)} fusion(f32[24,16,8,128]{3,2,1,0:T(8,128)} %fusion.138, f32[24,4,8,128]{3,2,1,0:T(8,128)S(1)} %collective-permute-done.9, f32[24,4,8,128]{3,2,1,0:T(8,128)S(1)} %collective-permute-done.8, f32[24,24,16,136]{3,2,1,0:T(8,128)} %select_maximum_fusion.6, f32[24,16,8,128]{3,2,1,0:T(8,128)} %copy-done.2, ...), kind=kLoop, calls=%fused_computation.234 | loop fusion | flops 17694720 | bytes 31589888 | tf_op jit(solution)/shard_map/add | solution.py:79
  320.1 5.0 collective-permute-start.11
  325.2 7.3 %collective-permute-done.10 = f32[24,4,8,128]{3,2,1,0:T(8,128)S(1)} collective-permute-done((f32[24,4,8,128]{3,2,1,0:T(8,128)S(1)}, f32[24,4,8,128]{3,2,1,0:T(8,128)S(1)}, u32[]{:S(2)}, u32[]{:S(2)}) %collective-permute-start.10) | collective-permute-done | bytes 393248 | tf_op jit(solution)/shard_map/ppermute | solution.py:17
  332.5 8.6 %collective-permute-done.11 = f32[24,4,8,128]{3,2,1,0:T(8,128)S(1)} collective-permute-done((f32[24,4,8,128]{3,2,1,0:T(8,128)S(1)}, f32[24,4,8,128]{3,2,1,0:T(8,128)S(1)}, u32[]{:S(2)}, u32[]{:S(2)}) %collective-permute-start.11) | collective-permute-done | bytes 393248 | tf_op jit(solution)/shard_map/ppermute | solution.py:16
  341.1 6.0 %select_maximum_fusion.4 = f32[24,24,16,136]{3,2,1,0:T(8,128)} fusion(f32[24,4,8,128]{3,2,1,0:T(8,128)S(1)} %collective-permute-done.10, f32[24,16,8,128]{3,2,1,0:T(8,128)S(1)} %fusion.107, f32[24,4,8,128]{3,2,1,0:T(8,128)S(1)} %collective-permute-done.11), kind=kLoop, calls=%fused_computation.24 | loop fusion | flops 18800640 | bytes 7372800 | tf_op jit(solution)/shard_map/concatenate | solution.py:18
  347.1 39.7 %fusion.76 = f32[24,16,8,128]{3,2,1,0:T(8,128)S(1)} fusion(f32[24,16,8,128]{3,2,1,0:T(8,128)} %copy-done.1, f32[24,4,8,128]{3,2,1,0:T(8,128)S(1)} %collective-permute-done.11, f32[24,4,8,128]{3,2,1,0:T(8,128)S(1)} %collective-permute-done.10, f32[24,24,16,136]{3,2,1,0:T(8,128)} %select_maximum_fusion.4, f32[24,16,8,128]{3,2,1,0:T(8,128)} %fusion.138, ...), kind=kLoop, calls=%fused_computation.203 | loop fusion | flops 17694720 | bytes 31589888 | tf_op jit(solution)/shard_map/add | solution.py:79
  389.1 5.3 collective-permute-start.13
  395.8 5.8 %collective-permute-done.12 = f32[24,4,8,128]{3,2,1,0:T(8,128)S(1)} collective-permute-done((f32[24,4,8,128]{3,2,1,0:T(8,128)}, f32[24,4,8,128]{3,2,1,0:T(8,128)S(1)}, u32[]{:S(2)}, u32[]{:S(2)}) %collective-permute-start.12) | collective-permute-done | bytes 393248 | tf_op jit(solution)/shard_map/ppermute | solution.py:17
  401.7 8.7 %collective-permute-done.13 = f32[24,4,8,128]{3,2,1,0:T(8,128)S(1)} collective-permute-done((f32[24,4,8,128]{3,2,1,0:T(8,128)}, f32[24,4,8,128]{3,2,1,0:T(8,128)S(1)}, u32[]{:S(2)}, u32[]{:S(2)}) %collective-permute-start.13) | collective-permute-done | bytes 393248 | tf_op jit(solution)/shard_map/ppermute | solution.py:16
  410.4 6.0 %select_maximum_fusion.2 = f32[24,24,16,136]{3,2,1,0:T(8,128)} fusion(f32[24,4,8,128]{3,2,1,0:T(8,128)S(1)} %collective-permute-done.12, f32[24,16,8,128]{3,2,1,0:T(8,128)S(1)} %fusion.76, f32[24,4,8,128]{3,2,1,0:T(8,128)S(1)} %collective-permute-done.13), kind=kLoop, calls=%fused_computation.22 | loop fusion | flops 18800640 | bytes 7372800 | tf_op jit(solution)/shard_map/concatenate | solution.py:18
  416.3 37.5 %fusion.45 = f32[24,16,8,128]{3,2,1,0:T(8,128)} fusion(f32[24,16,8,128]{3,2,1,0:T(8,128)S(1)} %fusion.76, f32[24,4,8,128]{3,2,1,0:T(8,128)S(1)} %collective-permute-done.13, f32[24,4,8,128]{3,2,1,0:T(8,128)S(1)} %collective-permute-done.12, f32[24,24,16,136]{3,2,1,0:T(8,128)} %select_maximum_fusion.2, f32[24,16,8,128]{3,2,1,0:T(8,128)} %copy-done.1, ...), kind=kLoop, calls=%fused_computation.172 | loop fusion | flops 17694720 | bytes 31589888 | tf_op jit(solution)/shard_map/add | solution.py:79
  456.4 4.9 collective-permute-start.15
  461.4 7.4 %collective-permute-done.14 = f32[24,4,8,128]{3,2,1,0:T(8,128)S(1)} collective-permute-done((f32[24,4,8,128]{3,2,1,0:T(8,128)S(1)}, f32[24,4,8,128]{3,2,1,0:T(8,128)S(1)}, u32[]{:S(2)}, u32[]{:S(2)}) %collective-permute-start.14) | collective-permute-done | bytes 393248 | tf_op jit(solution)/shard_map/ppermute | solution.py:17
  468.8 8.6 %collective-permute-done.15 = f32[24,4,8,128]{3,2,1,0:T(8,128)S(1)} collective-permute-done((f32[24,4,8,128]{3,2,1,0:T(8,128)S(1)}, f32[24,4,8,128]{3,2,1,0:T(8,128)S(1)}, u32[]{:S(2)}, u32[]{:S(2)}) %collective-permute-start.15) | collective-permute-done | bytes 393248 | tf_op jit(solution)/shard_map/ppermute | solution.py:16
  478.1 6.0 %select_maximum_fusion = f32[24,24,16,136]{3,2,1,0:T(8,128)} fusion(f32[24,4,8,128]{3,2,1,0:T(8,128)S(1)} %collective-permute-done.14, f32[24,16,8,128]{3,2,1,0:T(8,128)S(1)} %copy-done.6, f32[24,4,8,128]{3,2,1,0:T(8,128)S(1)} %collective-permute-done.15), kind=kLoop, calls=%fused_computation.20 | loop fusion | flops 18800640 | bytes 7372800 | tf_op jit(solution)/shard_map/concatenate | solution.py:18
  484.1 41.3 %fusion.265 = (bf16[24,16,8,128]{3,2,1,0:T(8,128)(2,1)S(1)}, f32[24,16,8,128]{3,2,1,0:T(8,128)}) fusion(f32[16,8,128]{2,1,0:T(8,128)S(1)} %copy.18, f32[24,16]{1,0:T(8,128)S(1)} %and_convert_fusion, bf16[24,16,8,128]{3,2,1,0:T(8,128)(2,1)S(1)} %copy-done, f32[24,24,16,136]{3,2,1,0:T(8,128)} %select_maximum_fusion, f32[24,16,8,128]{3,2,1,0:T(8,128)} %fusion.45, ...), kind=kLoop, calls=%fused_computation.448 | loop fusion | flops 18087936 | bytes 32376320 | tf_op jit(solution)/shard_map/convert_element_type | solution.py:86
  525.5 3.0 convolution_bitcast_fusion
  528.5 2.5 collective-permute-start.16
  530.9 1.7 collective-permute-done.16
  532.6 1.7 collective-permute-start.17
  534.3 2.0 collective-permute-done.17
  536.3 2.7 collective-permute-start.18
  539.0 1.9 collective-permute-done.18
  (67 shorter events, 17.4 us)
Async XLA Ops:
  7.2 31.3 %copy-start.13 = (s32[24,2]{0,1:T(2,128)S(1)}, s32[24,2]{0,1:T(2,128)}, u32[]{:S(2)}) copy-start(s32[24,2]{0,1:T(2,128)} %param.7) | copy-start | bytes 580
  7.2 518.3 %all-gather.2.cloned.1.call-start = ((), (), s32[]{:S(2)}) async-start(), calls=%async_computation | async-start | bytes 3932160 | tf_op jit(solution)/shard_map/all_gather | solution.py:88
  7.3 31.2 %collective-permute-start = (f32[24,4,8,128]{3,2,1,0:T(8,128)S(1)}, f32[24,4,8,128]{3,2,1,0:T(8,128)S(1)}, u32[]{:S(2)}, u32[]{:S(2)}) collective-permute-start(f32[24,4,8,128]{3,2,1,0:T(8,128)S(1)} %broadcast.90), channel_id=1, source_target_pairs={{1,0},{2,1},{3,2},{4,3},{5,4},{6,5},{7,6},{9,8},{10,9},{11,10},{12... | collective-permute-start | bytes 1179656 | tf_op jit(solution)/shard_map/ppermute | solution.py:17
  8.6 30.0 %collective-permute-start.1 = (f32[24,4,8,128]{3,2,1,0:T(8,128)S(1)}, f32[24,4,8,128]{3,2,1,0:T(8,128)S(1)}, u32[]{:S(2)}, u32[]{:S(2)}) collective-permute-start(f32[24,4,8,128]{3,2,1,0:T(8,128)S(1)} %broadcast.90), channel_id=1, source_target_pairs={{0,1},{1,2},{2,3},{3,4},{4,5},{5,6},{6,7},{8,9},{9,10},{10,11},{11... | collective-permute-start | bytes 1179656 | tf_op jit(solution)/shard_map/ppermute | solution.py:16
  38.5 1.1 copy-start
  38.5 1.1 copy-start.7
  43.6 22.6 %copy-start.5 = (f32[24,16,8,128]{3,2,1,0:T(8,128)}, f32[24,16,8,128]{3,2,1,0:T(8,128)S(1)}, u32[]{:S(2)}) copy-start(f32[24,16,8,128]{3,2,1,0:T(8,128)S(1)} %fusion.231) | copy-start | bytes 4718596
  43.7 13.9 %collective-permute-start.2 = (f32[24,4,8,128]{3,2,1,0:T(8,128)S(1)}, f32[24,4,8,128]{3,2,1,0:T(8,128)S(1)}, u32[]{:S(2)}, u32[]{:S(2)}) collective-permute-start(f32[24,4,8,128]{3,2,1,0:T(8,128)S(1)} %get-tuple-element.16), channel_id=1, source_target_pairs={{1,0},{2,1},{3,2},{4,3},{5,4},{6,5},{7,6},{9,8},{10,9},{11,10},{12... | collective-permute-start | bytes 1179656 | tf_op jit(solution)/shard_map/ppermute | solution.py:17
  45.0 21.2 %collective-permute-start.3 = (f32[24,4,8,128]{3,2,1,0:T(8,128)S(1)}, f32[24,4,8,128]{3,2,1,0:T(8,128)S(1)}, u32[]{:S(2)}, u32[]{:S(2)}) collective-permute-start(f32[24,4,8,128]{3,2,1,0:T(8,128)S(1)} %get-tuple-element.17), channel_id=1, source_target_pairs={{0,1},{1,2},{2,3},{3,4},{4,5},{5,6},{6,7},{8,9},{9,10},{10,11},{11... | collective-permute-start | bytes 1179656 | tf_op jit(solution)/shard_map/ppermute | solution.py:16
  112.7 22.5 %copy-start.4 = (f32[24,16,8,128]{3,2,1,0:T(8,128)}, f32[24,16,8,128]{3,2,1,0:T(8,128)S(1)}, u32[]{:S(2)}) copy-start(f32[24,16,8,128]{3,2,1,0:T(8,128)S(1)} %fusion.200) | copy-start | bytes 4718596
  112.7 6.5 %copy-start.12 = (f32[16,8,128]{2,0,1:T(8,128)S(1)}, f32[16,8,128]{2,0,1:T(8,128)}, u32[]{:S(2)}) copy-start(f32[16,8,128]{2,0,1:T(8,128)} %get-tuple-element.23) | copy-start | bytes 196612
  112.8 13.8 %collective-permute-start.4 = (f32[24,4,8,128]{3,2,1,0:T(8,128)S(1)}, f32[24,4,8,128]{3,2,1,0:T(8,128)S(1)}, u32[]{:S(2)}, u32[]{:S(2)}) collective-permute-start(f32[24,4,8,128]{3,2,1,0:T(8,128)S(1)} %get-tuple-element.14), channel_id=1, source_target_pairs={{1,0},{2,1},{3,2},{4,3},{5,4},{6,5},{7,6},{9,8},{10,9},{11,10},{12... | collective-permute-start | bytes 1179656 | tf_op jit(solution)/shard_map/ppermute | solution.py:17
  114.2 21.0 %collective-permute-start.5 = (f32[24,4,8,128]{3,2,1,0:T(8,128)S(1)}, f32[24,4,8,128]{3,2,1,0:T(8,128)S(1)}, u32[]{:S(2)}, u32[]{:S(2)}) collective-permute-start(f32[24,4,8,128]{3,2,1,0:T(8,128)S(1)} %get-tuple-element.15), channel_id=1, source_target_pairs={{0,1},{1,2},{2,3},{3,4},{4,5},{5,6},{6,7},{8,9},{9,10},{10,11},{11... | collective-permute-start | bytes 1179656 | tf_op jit(solution)/shard_map/ppermute | solution.py:16
  182.3 28.5 %copy-start.2 = (f32[24,16,8,128]{3,2,1,0:T(8,128)}, f32[24,16,8,128]{3,2,1,0:T(8,128)S(1)}, u32[]{:S(2)}) copy-start(f32[24,16,8,128]{3,2,1,0:T(8,128)S(1)} %fusion.169) | copy-start | bytes 4718596
  182.3 6.7 %copy-start.11 = (f32[16,8,128]{2,0,1:T(8,128)S(1)}, f32[16,8,128]{2,0,1:T(8,128)}, u32[]{:S(2)}) copy-start(f32[16,8,128]{2,0,1:T(8,128)} %get-tuple-element.22) | copy-start | bytes 196612
  182.4 13.8 %collective-permute-start.6 = (f32[24,4,8,128]{3,2,1,0:T(8,128)S(1)}, f32[24,4,8,128]{3,2,1,0:T(8,128)S(1)}, u32[]{:S(2)}, u32[]{:S(2)}) collective-permute-start(f32[24,4,8,128]{3,2,1,0:T(8,128)S(1)} %get-tuple-element.12), channel_id=1, source_target_pairs={{1,0},{2,1},{3,2},{4,3},{5,4},{6,5},{7,6},{9,8},{10,9},{11,10},{12... | collective-permute-start | bytes 1179656 | tf_op jit(solution)/shard_map/ppermute | solution.py:17
  183.8 21.0 %collective-permute-start.7 = (f32[24,4,8,128]{3,2,1,0:T(8,128)S(1)}, f32[24,4,8,128]{3,2,1,0:T(8,128)S(1)}, u32[]{:S(2)}, u32[]{:S(2)}) collective-permute-start(f32[24,4,8,128]{3,2,1,0:T(8,128)S(1)} %get-tuple-element.13), channel_id=1, source_target_pairs={{0,1},{1,2},{2,3},{3,4},{4,5},{5,6},{6,7},{8,9},{9,10},{10,11},{11... | collective-permute-start | bytes 1179656 | tf_op jit(solution)/shard_map/ppermute | solution.py:16
  248.4 23.6 %copy-start.3 = (f32[24,16,8,128]{3,2,1,0:T(8,128)S(1)}, f32[24,16,8,128]{3,2,1,0:T(8,128)}, u32[]{:S(2)}) copy-start(f32[24,16,8,128]{3,2,1,0:T(8,128)} %fusion.138) | copy-start | bytes 4718596
  249.7 13.7 %collective-permute-start.8 = (f32[24,4,8,128]{3,2,1,0:T(8,128)S(1)}, f32[24,4,8,128]{3,2,1,0:T(8,128)S(1)}, u32[]{:S(2)}, u32[]{:S(2)}) collective-permute-start(f32[24,4,8,128]{3,2,1,0:T(8,128)S(1)} %get-tuple-element.10), channel_id=1, source_target_pairs={{1,0},{2,1},{3,2},{4,3},{5,4},{6,5},{7,6},{9,8},{10,9},{11,10},{12... | collective-permute-start | bytes 1179656 | tf_op jit(solution)/shard_map/ppermute | solution.py:17
  251.0 21.0 %collective-permute-start.9 = (f32[24,4,8,128]{3,2,1,0:T(8,128)S(1)}, f32[24,4,8,128]{3,2,1,0:T(8,128)S(1)}, u32[]{:S(2)}, u32[]{:S(2)}) collective-permute-start(f32[24,4,8,128]{3,2,1,0:T(8,128)S(1)} %get-tuple-element.11), channel_id=1, source_target_pairs={{0,1},{1,2},{2,3},{3,4},{4,5},{5,6},{6,7},{8,9},{9,10},{10,11},{11... | collective-permute-start | bytes 1179656 | tf_op jit(solution)/shard_map/ppermute | solution.py:16
  318.8 22.3 %copy-start.1 = (f32[24,16,8,128]{3,2,1,0:T(8,128)}, f32[24,16,8,128]{3,2,1,0:T(8,128)S(1)}, u32[]{:S(2)}) copy-start(f32[24,16,8,128]{3,2,1,0:T(8,128)S(1)} %fusion.107) | copy-start | bytes 4718596
  318.8 13.7 %collective-permute-start.10 = (f32[24,4,8,128]{3,2,1,0:T(8,128)S(1)}, f32[24,4,8,128]{3,2,1,0:T(8,128)S(1)}, u32[]{:S(2)}, u32[]{:S(2)}) collective-permute-start(f32[24,4,8,128]{3,2,1,0:T(8,128)S(1)} %get-tuple-element.8), channel_id=1, source_target_pairs={{1,0},{2,1},{3,2},{4,3},{5,4},{6,5},{7,6},{9,8},{10,9},{11,10},{12... | collective-permute-start | bytes 1179656 | tf_op jit(solution)/shard_map/ppermute | solution.py:17
  320.1 21.0 %collective-permute-start.11 = (f32[24,4,8,128]{3,2,1,0:T(8,128)S(1)}, f32[24,4,8,128]{3,2,1,0:T(8,128)S(1)}, u32[]{:S(2)}, u32[]{:S(2)}) collective-permute-start(f32[24,4,8,128]{3,2,1,0:T(8,128)S(1)} %get-tuple-element.9), channel_id=1, source_target_pairs={{0,1},{1,2},{2,3},{3,4},{4,5},{5,6},{6,7},{8,9},{9,10},{10,11},{11... | collective-permute-start | bytes 1179656 | tf_op jit(solution)/shard_map/ppermute | solution.py:16
  386.8 7.5 %copy-start.10 = (bf16[24,16,8,128]{3,2,1,0:T(8,128)(2,1)S(1)}, bf16[24,16,8,128]{3,2,1,0:T(8,128)(2,1)}, u32[]{:S(2)}) copy-start(bf16[24,16,8,128]{3,2,1,0:T(8,128)(2,1)} %param.11) | copy-start | bytes 2359300
  387.8 13.9 %collective-permute-start.12 = (f32[24,4,8,128]{3,2,1,0:T(8,128)}, f32[24,4,8,128]{3,2,1,0:T(8,128)S(1)}, u32[]{:S(2)}, u32[]{:S(2)}) collective-permute-start(f32[24,4,8,128]{3,2,1,0:T(8,128)} %get-tuple-element.6), channel_id=1, source_target_pairs={{1,0},{2,1},{3,2},{4,3},{5,4},{6,5},{7,6},{9,8},{10,9},{11,10},{12... | collective-permute-start | bytes 1179656 | tf_op jit(solution)/shard_map/ppermute | solution.py:17
  389.1 21.3 %collective-permute-start.13 = (f32[24,4,8,128]{3,2,1,0:T(8,128)}, f32[24,4,8,128]{3,2,1,0:T(8,128)S(1)}, u32[]{:S(2)}, u32[]{:S(2)}) collective-permute-start(f32[24,4,8,128]{3,2,1,0:T(8,128)} %get-tuple-element.7), channel_id=1, source_target_pairs={{0,1},{1,2},{2,3},{3,4},{4,5},{5,6},{6,7},{8,9},{9,10},{10,11},{11... | collective-permute-start | bytes 1179656 | tf_op jit(solution)/shard_map/ppermute | solution.py:16
  453.8 24.3 %copy-start.6 = (f32[24,16,8,128]{3,2,1,0:T(8,128)S(1)}, f32[24,16,8,128]{3,2,1,0:T(8,128)}, u32[]{:S(2)}) copy-start(f32[24,16,8,128]{3,2,1,0:T(8,128)} %fusion.45) | copy-start | bytes 4718596
  455.1 13.7 %collective-permute-start.14 = (f32[24,4,8,128]{3,2,1,0:T(8,128)S(1)}, f32[24,4,8,128]{3,2,1,0:T(8,128)S(1)}, u32[]{:S(2)}, u32[]{:S(2)}) collective-permute-start(f32[24,4,8,128]{3,2,1,0:T(8,128)S(1)} %get-tuple-element.5), channel_id=1, source_target_pairs={{1,0},{2,1},{3,2},{4,3},{5,4},{6,5},{7,6},{9,8},{10,9},{11,10},{12... | collective-permute-start | bytes 1179656 | tf_op jit(solution)/shard_map/ppermute | solution.py:17
  456.4 21.0 %collective-permute-start.15 = (f32[24,4,8,128]{3,2,1,0:T(8,128)S(1)}, f32[24,4,8,128]{3,2,1,0:T(8,128)S(1)}, u32[]{:S(2)}, u32[]{:S(2)}) collective-permute-start(f32[24,4,8,128]{3,2,1,0:T(8,128)S(1)} %get-tuple-element.4), channel_id=1, source_target_pairs={{0,1},{1,2},{2,3},{3,4},{4,5},{5,6},{6,7},{8,9},{9,10},{10,11},{11... | collective-permute-start | bytes 1179656 | tf_op jit(solution)/shard_map/ppermute | solution.py:16
  468.8 8.6 %copy-start.8 = (f32[24,4,8,128]{3,2,1,0:T(8,128)}, f32[24,4,8,128]{3,2,1,0:T(8,128)S(1)}, u32[]{:S(2)}) copy-start(f32[24,4,8,128]{3,2,1,0:T(8,128)S(1)} %collective-permute-done.14) | copy-start | bytes 1179652
  477.4 0.8 copy-start.9
  528.5 4.2 collective-permute-start.16
  532.6 3.7 collective-permute-start.17
  536.3 4.6 collective-permute-start.18
Sparse Core Ops, SparseCore 0:
  395.9 30.1 all-gather.1
